TPU v7x, 32 devices: a whole 2x2x4 slice. The times are simulated.
32 devices in a mesh: groups: 2 (over y), seq: 1, mp: 8 (over z, x), section: 2 (over core).
Axes of the slice: x: 2, y: 2, z: 4, core: 2. Of those that a mesh axis runs over, the one named last changes fastest.
Arguments:
- latent: bfloat16 [1024, 3072], P(('groups', 'seq', 'section'), 'mp'), parts along dimension 0, may hold values from -6 to 6
- t_index: int32 [2], P('groups'), parts along dimension 0, may hold values from 0 to 27
- mod_table: bfloat16 [28, 3, 3072], P(None, None, 'mp'), may hold values from -1 to 4
- w_qkv: bfloat16 [3072, 6144], P('section', 'mp'), may hold values from -1 to 1
- w_out: bfloat16 [2048, 3072], P('section', 'mp'), may hold values from -0.125 to 0.125
Outputs:
- updated: bfloat16 [1024, 3072], P(('groups', 'seq', 'section'), 'mp'), parts along dimension 0
There are 2 independent parts, one for each index of `groups`. A program takes and returns all parts, laid end to end along the dimension named above; an argument that names none is the same for every part. Nothing has to cross between parts.
Inputs may be any that keep to these rules, and one draw needn't show every extreme that they name: `t_index`: the index of the current step among 28.
All inputs are finite; a program needn't handle non-finite values.
Results may differ from a plain program's by a relative error of at most 0.0085.
The roundings to bfloat16 on the way count: a program that leaves them out, or rounds other values in their place, can miss the bound.
Values may be sent and summed in bfloat16 or wider, within the bound.
A program may use at most 128 MiB of HBM per device.

v0:
```python
import math

import jax
import jax.numpy as jnp
from jax import lax
from jax.sharding import PartitionSpec as P

HEAD_DIM = 128


def layer_normed(values):
    mean_row = jnp.mean(values, axis=-1, keepdims=True)
    centred = values - mean_row
    variance = jnp.mean(centred * centred, axis=-1, keepdims=True)
    return centred * lax.rsqrt(variance + 1e-06)


def local(latent, t_index, mod_table, w_qkv, w_out):
    mod_local = lax.dynamic_index_in_dim(mod_table, t_index[0], 0, keepdims=False)
    features, mod_whole = (
        lax.all_gather(latent, "mp", axis=1, tiled=True),
        lax.all_gather(mod_local, "mp", axis=1, tiled=True),
    )
    mod_float = mod_whole.astype(jnp.float32)
    modulated = (
        layer_normed(features.astype(jnp.float32)) * (1.0 + mod_float[1]) + mod_float[0]
    ).astype(jnp.bfloat16)
    tok_rows = latent.shape[0]
    heads_dev = w_qkv.shape[1] // (3 * HEAD_DIM)
    qkv_full, out_full = (
        lax.all_gather(w_qkv, "section", axis=0, tiled=True),
        lax.all_gather(w_out, "section", axis=0, tiled=True),
    )
    projected = jnp.dot(modulated, qkv_full, preferred_element_type=jnp.float32).astype(
        jnp.bfloat16
    )
    grouped = projected.reshape(tok_rows, heads_dev, 3, HEAD_DIM)
    queries = grouped[:, :, 0]
    key_rows = grouped[:, :, 1]
    value_rows = grouped[:, :, 2]
    scale_factor = 1.0 / math.sqrt(HEAD_DIM)
    initial = (
        jnp.full((tok_rows, heads_dev), -1e30, jnp.float32),
        jnp.zeros((tok_rows, heads_dev), jnp.float32),
        jnp.zeros((tok_rows, heads_dev, HEAD_DIM), jnp.float32),
    )
    key_piece = lax.all_gather(key_rows, ("seq", "section"), axis=0, tiled=True)
    value_piece = lax.all_gather(value_rows, ("seq", "section"), axis=0, tiled=True)
    total_rows = key_piece.shape[0]
    block_rows = math.gcd(total_rows, 1024)

    def one_block(block_index, carried_block):
        running, totals, weighted = carried_block
        key_block = lax.dynamic_slice_in_dim(key_piece, block_index * block_rows, block_rows, 0)
        value_block = lax.dynamic_slice_in_dim(value_piece, block_index * block_rows, block_rows, 0)
        scores = (
            jnp.einsum("thd,khd->thk", queries, key_block, preferred_element_type=jnp.float32)
            * scale_factor
        )
        newest = jnp.maximum(running, jnp.max(scores, axis=-1))
        factor = jnp.exp(running - newest)
        weights = jnp.exp(scores - newest[..., None])
        totals = totals * factor + jnp.sum(weights, axis=-1)
        weighted = weighted * factor[..., None] + jnp.einsum(
            "thk,khd->thd",
            weights.astype(jnp.bfloat16),
            value_block,
            preferred_element_type=jnp.float32,
        )
        return (newest, totals, weighted)

    finished = lax.fori_loop(0, total_rows // block_rows, one_block, initial)
    attended = (
        (finished[2] / finished[1][..., None])
        .astype(jnp.bfloat16)
        .reshape(tok_rows, heads_dev * HEAD_DIM)
    )
    mixed_rows = jnp.dot(
        lax.all_gather(attended, "mp", axis=1, tiled=True),
        out_full,
        preferred_element_type=jnp.float32,
    )
    return (latent.astype(jnp.float32) + mod_local[2].astype(jnp.float32) * mixed_rows).astype(
        jnp.bfloat16
    )


def solution(mesh):
    in_specs = (
        P(("groups", "seq", "section"), "mp"),
        P("groups"),
        P(None, None, "mp"),
        P("section", "mp"),
        P("section", "mp"),
    )
    out_specs = P(("groups", "seq", "section"), "mp")
    return jax.shard_map(local, mesh=mesh, in_specs=in_specs, out_specs=out_specs, check_vma=False)
```

profile of v0, /device:TPU:0, one launch (start us, length us, event | category | flops | bytes accessed | tf_op | source)
XLA Modules:
  0.0 136.6 jit_solution(5764372131520535393)
XLA Ops:
  6.5 0.7 all-gather.8.cloned.1.call-update
  7.3 0.0 all-gather.10.cloned.1.call-start
  7.3 0.7 all-gather.10.cloned.1.call-update
  8.0 0.0 all-gather.14.cloned.1.call-start
  8.1 0.7 all-gather.14.cloned.1.call-update
  8.7 0.0 all-gather.12.cloned.1.call-start
  9.4 0.7 constant_dynamic-slice_fusion
  10.2 28.0 %all-gather = bf16[1,3,3072]{2,0,1:T(2,128)(2,1)S(1)} all-gather(bf16[1,3,384]{2,0,1:T(2,128)(2,1)S(1)} %constant_dynamic-slice_fusion), channel_id=2, replica_groups=mesh['groups'=2,'seq'=1,'mp'=8,'section'=2] {'mp'}, dimensions={2}, use_global_device_ids=true | all-gather | bytes 20736 | tf_op jit(solution)/shard_map/all_gather | solution.py:22
  38.3 18.4 %all-gather.8.cloned.1.call-done = bf16[256,3072]{1,0:T(8,128)(2,1)} async-done(((bf16[256,384]{1,0:T(8,128)(2,1)}), bf16[256,3072]{1,0:T(8,128)(2,1)}) %all-gather.8.cloned.1.call-update) | async-done | bytes 1572880 | tf_op jit(solution)/shard_map/all_gather | solution.py:21
  56.7 1.8 %convert_reduce_fusion = f32[256]{0:T(256)S(1)} fusion(bf16[256,3072]{1,0:T(8,128)(2,1)} %all-gather.8.cloned.1.call-done), kind=kLoop, calls=%fused_computation.1 | loop fusion | flops 1572608 | bytes 1573888 | tf_op jit(solution)/shard_map/reduce_sum | solution.py:12
  58.5 2.0 %fusion.2 = f32[256]{0:T(256)S(1)} fusion(bf16[256,3072]{1,0:T(8,128)(2,1)} %all-gather.8.cloned.1.call-done, f32[256]{0:T(256)S(1)} %broadcast_multiply_fusion), kind=kLoop, calls=%fused_computation.4 | loop fusion | flops 3145472 | bytes 1574912 | tf_op jit(solution)/shard_map/reduce_sum | solution.py:14
  60.5 10.4 %all-gather.10.cloned.1.call-done = bf16[3072,768]{1,0:T(8,128)(2,1)} async-done(((bf16[1536,768]{1,0:T(8,128)(2,1)}), bf16[3072,768]{1,0:T(8,128)(2,1)}) %all-gather.10.cloned.1.call-update) | async-done | bytes 4718608 | tf_op jit(solution)/shard_map/all_gather | solution.py:31
  70.8 3.9 %fusion.13 = bf16[256,768]{1,0:T(8,128)(2,1)S(1)} fusion(bf16[3072,768]{1,0:T(8,128)(2,1)} %all-gather.10.cloned.1.call-done, bf16[256,3072]{1,0:T(8,128)(2,1)S(1)} %copy-done, f32[3072]{0:T(1024)S(1)} %bitcast.40, f32[3072]{0:T(1024)S(1)} %bitcast.41, f32[256]{0:T(256)S(1)} %add_rsqrt_fusion, f32[256]{0:T(256)S(1)} %broadcast_multiply_fusion), kind=kOutput, calls=%fused_computation.15 | convolution fusion | flops 1212874752 | bytes 6711296 | tf_op jit(solution)/shard_map/dot_general | solution.py:34
  74.8 0.2 copy.10
  75.0 0.1 copy.16
  75.1 2.0 %all-gather.1 = bf16[512,2,1,128]{3,0,1,2:T(8,128)(2,1)S(1)} all-gather(bf16[256,2,1,128]{3,0,1,2:T(8,128)(2,1)S(1)} %copy.16), channel_id=3, replica_groups=mesh['groups'=2,'seq'=1,'mp'=8,'section'=2] {'seq','section'}, dimensions={0}, use_global_device_ids=true | all-gather | bytes 393216 | tf_op jit(solution)/shard_map/all_gather | solution.py:47
  77.1 2.0 %all-gather.2 = bf16[512,2,1,128]{0,3,1,2:T(8,128)(2,1)S(1)} all-gather(bf16[256,2,1,128]{0,3,1,2:T(8,128)(2,1)S(1)} %get-tuple-element.19), channel_id=4, replica_groups=mesh['groups'=2,'seq'=1,'mp'=8,'section'=2] {'seq','section'}, dimensions={0}, use_global_device_ids=true | all-gather | bytes 393216 | tf_op jit(solution)/shard_map/all_gather | solution.py:48
  79.1 0.3 fusion.29
  79.4 0.2 fusion.21
  79.6 1.0 fusion.20
  80.6 0.7 fusion.27
  81.3 2.1 %all-gather.14.cloned.1.call-done = bf16[2048,384]{1,0:T(8,128)(2,1)} async-done(((bf16[1024,384]{1,0:T(8,128)(2,1)}), bf16[2048,384]{1,0:T(8,128)(2,1)}) %all-gather.14.cloned.1.call-update) | async-done | bytes 1572880 | tf_op jit(solution)/shard_map/all_gather | solution.py:32
  83.4 43.5 %all-gather.12.cloned.1.call-done = bf16[256,2048]{0,1:T(8,128)(2,1)} async-done(((bf16[256,256]{0,1:T(8,128)(2,1)}), bf16[256,2048]{0,1:T(8,128)(2,1)}) %all-gather.12.cloned.1.call-update) | async-done | bytes 1048592 | tf_op jit(solution)/shard_map/all_gather | solution.py:79
  126.9 3.2 %fusion.17 = bf16[256,384]{1,0:T(8,128)(2,1)} fusion(bf16[256,2048]{0,1:T(8,128)(2,1)} %all-gather.12.cloned.1.call-done, bf16[2048,384]{1,0:T(8,128)(2,1)} %all-gather.14.cloned.1.call-done, bf16[256,384]{1,0:T(8,128)(2,1)S(1)} %copy-done.1, f32[384]{0:T(512)S(1)} %fusion.27), kind=kOutput, calls=%fused_computation.18 | convolution fusion | flops 403046400 | bytes 3016192 | tf_op jit(solution)/shard_map/dot_general | solution.py:78
  (14 shorter events, 0.1 us)
Async XLA Ops:
  6.5 50.1 %all-gather.8.cloned.1.call-start = ((), (), s32[]{:S(2)}) async-start(), calls=%async_computation | async-start | bytes 1769472 | tf_op jit(solution)/shard_map/all_gather | solution.py:21
  7.3 63.6 %all-gather.10.cloned.1.call-start = ((), (), s32[]{:S(2)}) async-start(), calls=%async_computation.1 | async-start | bytes 7077888 | tf_op jit(solution)/shard_map/all_gather | solution.py:31
  8.0 75.4 %all-gather.14.cloned.1.call-start = ((), (), s32[]{:S(2)}) async-start(), calls=%async_computation.3 | async-start | bytes 2359296 | tf_op jit(solution)/shard_map/all_gather | solution.py:32
  8.7 118.1 %all-gather.12.cloned.1.call-start = ((), (), s32[]{:S(2)}) async-start(), calls=%async_computation.2 | async-start | bytes 1179648 | tf_op jit(solution)/shard_map/all_gather | solution.py:79
  56.7 14.2 %copy-start = (bf16[256,3072]{1,0:T(8,128)(2,1)S(1)}, bf16[256,3072]{1,0:T(8,128)(2,1)}, u32[]{:S(2)}) copy-start(bf16[256,3072]{1,0:T(8,128)(2,1)} %all-gather.8.cloned.1.call-done) | copy-start | bytes 4718596
  75.0 51.9 %copy-start.1 = (bf16[256,384]{1,0:T(8,128)(2,1)S(1)}, bf16[256,384]{1,0:T(8,128)(2,1)}, u32[]{:S(2)}) copy-start(bf16[256,384]{1,0:T(8,128)(2,1)} %param.5) | copy-start | bytes 589828
Sparse Core Ops, SparseCore 0:
  9.4 47.2 all-gather.7
  58.2 12.6 all-gather.9
  72.4 10.9 all-gather.13
  85.4 41.4 all-gather.11
where the time goes:
time: 137 us
  waiting for transfers between devices  76.4 us (56%)
  blocking collectives  32 us (23%)
  between operations  13.9 us (10%)
  matrix products  8.38 us (6%)
  other arithmetic  4.74 us (3%)
    all_gather x1, waiting for transfers between devices, local(): lax.all_gather(attended, 'mp', axis=1, tiled=True)  43.5 us
    all_gather x1, blocking collectives, local(): lax.all_gather(mod_local, 'mp', axis=1, tiled=True)  28 us
    all_gather x1, waiting for transfers between devices, local(): lax.all_gather(latent, 'mp', axis=1, tiled=True)  18.4 us
    all_gather x1, waiting for transfers between devices, local(): lax.all_gather(w_qkv, 'section', axis=0, tiled=True)  10.4 us
    dot_general x1, matrix products, local(): jnp.dot(modulated, qkv_full, preferred_element_type=jnp.float32)  3.95 us
    dot_general x1, matrix products, local(): jnp.dot(lax.all_gather(attended, 'mp', axis=1, tiled=True), out_full, pre...  3.15 us
  transfers between devices with their start and end apart: 4, of which 4 were waited for; matrix products, arithmetic and copies ran while one was open for 8% of the time, Pallas kernels for 0%

commit v1 on v0

--- a/solution.py
+++ b/solution.py
@@ -1,11 +1,17 @@
+import functools
 import math
 
 import jax
 import jax.numpy as jnp
 from jax import lax
+from jax.experimental import pallas as pl
+from jax.experimental.pallas import tpu as pltpu
 from jax.sharding import PartitionSpec as P
 
 HEAD_DIM = 128
+LANES = 128
+WIDE = 2
+MESH = pl.DeviceIdType.MESH
 
 
 def layer_normed(values):
@@ -85,6 +91,375 @@
     )
 
 
+def fused_kernel(
+    n,
+    x_hbm,
+    t_ref,
+    mod_ref,
+    wq_hbm,
+    wo_hbm,
+    out_ref,
+    xs,
+    small,
+    wq,
+    wo,
+    acc,
+    stat,
+    proj,
+    pkv,
+    att,
+    mixed,
+    own_sem,
+    ssem,
+    rsem,
+    small_send,
+    small_recv,
+    wq_sem,
+    wq_send,
+    wo_sem,
+    wo_send,
+    kv_send,
+    kv_recv,
+):
+    me = lax.axis_index("mp")
+    sec = lax.axis_index("section")
+    other = 1 - sec
+    deep = n // WIDE
+    z, x = me // WIDE, me % WIDE
+    rows, feats = x_hbm.shape
+    half = rows // 2
+    piece_q = wq.shape[1]
+    per_sec = n // 2
+    piece_o = wo.shape[1]
+    heads = att.shape[2] // HEAD_DIM
+
+    own_copy = pltpu.make_async_copy(x_hbm, xs.at[me], own_sem)
+    own_copy.start()
+
+    barrier = pltpu.get_barrier_semaphore()
+    for step in range(1, n):
+        pl.semaphore_signal(
+            barrier, inc=1, device_id={"mp": lax.rem(me + step, n)}, device_id_type=MESH
+        )
+    pl.semaphore_signal(barrier, inc=1, device_id={"section": other}, device_id_type=MESH)
+
+    def wq_local(i):
+        p = sec * per_sec + i
+        return pltpu.make_async_copy(
+            wq_hbm.at[pl.ds(i * piece_q, piece_q)], wq.at[p], wq_sem.at[p]
+        )
+
+    def wo_local(i):
+        return pltpu.make_async_copy(
+            wo_hbm.at[pl.ds(i * piece_o, piece_o)],
+            wo.at[sec * per_sec + i],
+            wo_sem.at[sec * per_sec + i],
+        )
+
+    for i in range(per_sec):
+        wq_local(i).start()
+    for i in range(per_sec):
+        wo_local(i).start()
+
+    own_copy.wait()
+    mine = xs[me].astype(jnp.float32)
+    mod_f = mod_ref[t_ref[0]].astype(jnp.float32)
+    mean_col = jnp.sum(mine, axis=1, keepdims=True) * (1.0 / feats)
+    off = mine - mean_col
+    m2_col = jnp.sum(off * off, axis=1, keepdims=True)
+    mean_row = jnp.broadcast_to(mean_col, (rows, LANES)).T[0:1, :]
+    m2_row = jnp.broadcast_to(m2_col, (rows, LANES)).T[0:1, :]
+    small[me, 0:1, :] = mod_f[0:1]
+    small[me, 1:2, :] = 1.0 + mod_f[1:2]
+    small[me, 2:3, 0:rows] = mean_row
+    small[me, 3:4, 0:rows] = m2_row
+
+    pl.semaphore_wait(barrier, n)
+
+    def small_copy(step):
+        return pltpu.make_async_remote_copy(
+            src_ref=small.at[me],
+            dst_ref=small.at[me],
+            send_sem=small_send.at[step],
+            recv_sem=small_recv.at[me],
+            device_id={"mp": lax.rem(me + step, n)},
+            device_id_type=MESH,
+        )
+
+    def chunk(phase, src, h):
+        if phase == 0:
+            return xs.at[src, pl.ds(h * half, half), :]
+        return att.at[src, :, pl.ds(h * HEAD_DIM, HEAD_DIM)]
+
+    def route(src, h):
+        sz, sx = src // WIDE, src % WIDE
+        same = sx == x
+        if h == 0:
+            first = jnp.bool_(False)
+        else:
+            first = jnp.logical_or(sz == 0, sz == deep - 1)
+        flow = jnp.logical_or(same, first)
+        up = jnp.logical_and(flow, jnp.logical_and(sz <= z, z + 1 < deep))
+        down = jnp.logical_and(flow, jnp.logical_and(sz >= z, z > 0))
+        across = jnp.logical_and(
+            same, jnp.logical_or(jnp.logical_not(first), sz == z)
+        )
+        return (
+            (0, up, me + WIDE),
+            (1, down, me - WIDE),
+            (2, across, z * WIDE + (1 - x)),
+        )
+
+    def hop(phase, src, h, direction, target):
+        return pltpu.make_async_remote_copy(
+            src_ref=chunk(phase, src, h),
+            dst_ref=chunk(phase, src, h),
+            send_sem=ssem.at[phase, direction, src, h],
+            recv_sem=rsem.at[phase, src, h],
+            device_id={"mp": target},
+            device_id_type=MESH,
+        )
+
+    def relay(phase, src, h):
+        for direction, wanted, target in route(src, h):
+
+            @pl.when(wanted)
+            def _():
+                hop(phase, src, h, direction, target).start()
+
+    def arrive(phase, src, h):
+        hop(phase, src, h, 0, me).wait_recv()
+        relay(phase, src, h)
+
+    for h in range(2):
+        relay(0, me, h)
+        if h == 0:
+            for step in range(1, n):
+                small_copy(step).start()
+
+    def wq_remote(i):
+        p = sec * per_sec + i
+        return pltpu.make_async_remote_copy(
+            src_ref=wq_hbm.at[pl.ds(i * piece_q, piece_q)],
+            dst_ref=wq.at[p],
+            send_sem=wq_send.at[i],
+            recv_sem=wq_sem.at[p],
+            device_id={"section": other},
+            device_id_type=MESH,
+        )
+
+    def wo_remote(i):
+        p = sec * per_sec + i
+        return pltpu.make_async_remote_copy(
+            src_ref=wo_hbm.at[pl.ds(i * piece_o, piece_o)],
+            dst_ref=wo.at[p],
+            send_sem=wo_send.at[i],
+            recv_sem=wo_sem.at[p],
+            device_id={"section": other},
+            device_id_type=MESH,
+        )
+
+    for i in range(per_sec):
+        wq_remote(i).start()
+    for i in range(per_sec):
+        wo_remote(i).start()
+
+    for step in range(1, n):
+        p = lax.rem(me + step, n)
+        pltpu.make_async_copy(small.at[p], small.at[p], small_recv.at[p]).wait()
+    total = jnp.zeros((1, rows), jnp.float32)
+    for p in range(n):
+        total = total + small[p, 2:3, 0:rows]
+    grand = total * (1.0 / n)
+    m2 = jnp.zeros((1, rows), jnp.float32)
+    for p in range(n):
+        gap = small[p, 2:3, 0:rows] - grand
+        m2 = m2 + small[p, 3:4, 0:rows] + feats * (gap * gap)
+    inv = lax.rsqrt(m2 * (1.0 / (n * feats)) + 1e-06)
+    stat[0] = jnp.broadcast_to(grand, (LANES, rows)).T
+    stat[1] = jnp.broadcast_to(inv, (LANES, rows)).T
+
+    def project(src):
+        pltpu.make_async_copy(wq.at[src], wq.at[src], wq_sem.at[src]).wait()
+        mean, rstd = stat[0], stat[1]
+        shift_scale = small[src, 0:2, :]
+        parts = []
+        for c in range(feats // LANES):
+            cols = slice(c * LANES, (c + 1) * LANES)
+            values = xs[src, :, cols].astype(jnp.float32)
+            parts.append(
+                ((values - mean) * rstd * shift_scale[1:2, cols] + shift_scale[0:1, cols]).astype(
+                    jnp.bfloat16
+                )
+            )
+        return jnp.dot(
+            jnp.concatenate(parts, axis=1), wq[src], preferred_element_type=jnp.float32
+        )
+
+    acc[...] = project(me)
+
+    def sweep(phase, use):
+        def body(d, carry):
+            where = []
+            for col in (True, False):
+                for sign in (1, -1):
+                    sz = z + sign * (d if col else d - 1)
+                    there = jnp.logical_and(sz >= 0, sz < deep)
+                    if not col and sign < 0:
+                        there = jnp.logical_and(there, d > 1)
+                    where.append((sz * WIDE + (x if col else 1 - x), there))
+            for h in range(2):
+                for src, there in where:
+
+                    @pl.when(there)
+                    def _():
+                        arrive(phase, src, h)
+
+            def one(i, carry_in):
+                col = i < 2
+                sign = 1 - 2 * lax.rem(i, 2)
+                sz = z + sign * jnp.where(col, d, d - 1)
+                there = jnp.logical_and(sz >= 0, sz < deep)
+                there = jnp.logical_and(there, jnp.logical_or(i < 3, d > 1))
+                src = sz * WIDE + jnp.where(col, x, 1 - x)
+
+                @pl.when(there)
+                def _():
+                    use(src)
+
+                return carry_in
+
+            return lax.fori_loop(0, 4, one, carry)
+
+        lax.fori_loop(1, deep + 1, body, 0)
+
+    def use_projection(src):
+        acc[...] += project(src)
+
+    sweep(0, use_projection)
+
+    def kv_copy(h):
+        return pltpu.make_async_remote_copy(
+            src_ref=proj.at[:, pl.ds((3 * h + 1) * HEAD_DIM, 2 * HEAD_DIM)],
+            dst_ref=pkv.at[h],
+            send_sem=kv_send.at[h],
+            recv_sem=kv_recv.at[h],
+            device_id={"section": other},
+            device_id_type=MESH,
+        )
+
+    for h in range(heads):
+        cols = slice((3 * h + 1) * HEAD_DIM, (3 * h + 3) * HEAD_DIM)
+        proj[:, cols] = acc[:, cols].astype(jnp.bfloat16)
+        kv_copy(h).start()
+
+    factor = 1.0 / math.sqrt(HEAD_DIM)
+    contract = (((1,), (1,)), ((), ()))
+    for h in range(heads):
+        base = 3 * h * HEAD_DIM
+        queries = acc[:, base : base + HEAD_DIM].astype(jnp.bfloat16)
+        own_k = proj[:, base + HEAD_DIM : base + 2 * HEAD_DIM]
+        own_v = proj[:, base + 2 * HEAD_DIM : base + 3 * HEAD_DIM]
+        s_own = lax.dot_general(queries, own_k, contract, preferred_element_type=jnp.float32) * factor
+        kv_copy(h).wait_recv()
+        far_k = pkv[h, :, 0:HEAD_DIM]
+        far_v = pkv[h, :, HEAD_DIM : 2 * HEAD_DIM]
+        s_far = lax.dot_general(queries, far_k, contract, preferred_element_type=jnp.float32) * factor
+        top = jnp.maximum(
+            jnp.max(s_own, axis=1, keepdims=True), jnp.max(s_far, axis=1, keepdims=True)
+        )
+        e_own = jnp.exp(s_own - top)
+        e_far = jnp.exp(s_far - top)
+        norm = jnp.sum(e_own, axis=1, keepdims=True) + jnp.sum(e_far, axis=1, keepdims=True)
+        weighted = jnp.dot(
+            e_own.astype(jnp.bfloat16), own_v, preferred_element_type=jnp.float32
+        ) + jnp.dot(e_far.astype(jnp.bfloat16), far_v, preferred_element_type=jnp.float32)
+        att[me, :, h * HEAD_DIM : (h + 1) * HEAD_DIM] = (weighted / norm).astype(jnp.bfloat16)
+        relay(1, me, h)
+
+    def mix(src):
+        pltpu.make_async_copy(wo.at[src], wo.at[src], wo_sem.at[src]).wait()
+        return jnp.dot(att[src], wo[src], preferred_element_type=jnp.float32)
+
+    mixed[...] = mix(me)
+
+    def use_mix(src):
+        mixed[...] += mix(src)
+
+    sweep(1, use_mix)
+
+    gate = mod_ref[t_ref[0]].astype(jnp.float32)[2:3]
+    out_ref[...] = (xs[me].astype(jnp.float32) + gate * mixed[...]).astype(jnp.bfloat16)
+
+    for step in range(1, n):
+        small_copy(step).wait_send()
+    for i in range(per_sec):
+        wq_remote(i).wait_send()
+        wo_remote(i).wait_send()
+    for h in range(heads):
+        kv_copy(h).wait_send()
+
+    def drain(src, carry):
+        for phase in range(2):
+            for h in range(2):
+                for direction, wanted, target in route(src, h):
+
+                    @pl.when(wanted)
+                    def _():
+                        hop(phase, src, h, direction, target).wait_send()
+
+        return carry
+
+    lax.fori_loop(0, n, drain, 0)
+
+
+def fused(n, latent, t_index, mod_table, w_qkv, w_out):
+    rows, feats = latent.shape
+    depth, cols = w_qkv.shape
+    depth_o, cols_o = w_out.shape
+    heads = cols // (3 * HEAD_DIM)
+    bf, f32 = jnp.bfloat16, jnp.float32
+    dma = pltpu.SemaphoreType.DMA
+    return pl.pallas_call(
+        functools.partial(fused_kernel, n),
+        out_shape=jax.ShapeDtypeStruct((rows, feats), bf),
+        in_specs=[
+            pl.BlockSpec(memory_space=pl.ANY),
+            pl.BlockSpec(memory_space=pltpu.SMEM),
+            pl.BlockSpec(memory_space=pltpu.VMEM),
+            pl.BlockSpec(memory_space=pl.ANY),
+            pl.BlockSpec(memory_space=pl.ANY),
+        ],
+        out_specs=pl.BlockSpec(memory_space=pltpu.VMEM),
+        scratch_shapes=[
+            pltpu.VMEM((n, rows, feats), bf),
+            pltpu.VMEM((n, 8, feats), f32),
+            pltpu.VMEM((n, 2 * depth // n, cols), bf),
+            pltpu.VMEM((n, 2 * depth_o // n, cols_o), bf),
+            pltpu.VMEM((rows, cols), f32),
+            pltpu.VMEM((2, rows, LANES), f32),
+            pltpu.VMEM((rows, cols), bf),
+            pltpu.VMEM((heads, rows, 2 * HEAD_DIM), bf),
+            pltpu.VMEM((n, rows, heads * HEAD_DIM), bf),
+            pltpu.VMEM((rows, cols_o), f32),
+            dma,
+            dma((2, 3, n, 2)),
+            dma((2, n, 2)),
+            dma((n,)),
+            dma((n,)),
+            dma((n,)),
+            dma((n // 2,)),
+            dma((n,)),
+            dma((n // 2,)),
+            dma((heads,)),
+            dma((heads,)),
+        ],
+        compiler_params=pltpu.CompilerParams(
+            collective_id=0, has_side_effects=True, vmem_limit_bytes=48 * 1024 * 1024
+        ),
+    )(latent, t_index, mod_table, w_qkv, w_out)
+
+
 def solution(mesh):
     in_specs = (
         P(("groups", "seq", "section"), "mp"),
@@ -94,4 +469,21 @@
         P("section", "mp"),
     )
     out_specs = P(("groups", "seq", "section"), "mp")
-    return jax.shard_map(local, mesh=mesh, in_specs=in_specs, out_specs=out_specs, check_vma=False)
+    n = mesh.shape["mp"]
+
+    def body(latent, t_index, mod_table, w_qkv, w_out):
+        heads = w_qkv.shape[1] // (3 * HEAD_DIM)
+        fits = (
+            mesh.shape["seq"] == 1
+            and mesh.shape["section"] == 2
+            and n % WIDE == 0
+            and n > WIDE
+            and heads == 2
+            and latent.shape[0] <= latent.shape[1]
+            and latent.shape[0] % 256 == 0
+        )
+        if not fits:
+            return local(latent, t_index, mod_table, w_qkv, w_out)
+        return fused(n, latent, t_index, mod_table, w_qkv, w_out)
+
+    return jax.shard_map(body, mesh=mesh, in_specs=in_specs, out_specs=out_specs, check_vma=False)

time: 137 us -> 52.5 us (0.38)
  waiting for transfers between devices: 76.4 us -> 0 us
  Pallas kernels: 0 us -> 46.3 us
  blocking collectives: 32 us -> 0 us
  between operations: 13.9 us -> 0.67 us
  matrix products: 8.38 us -> 0 us
  other arithmetic: 4.74 us -> 0 us
  local copies, waits for them, and re-layouts: 1.07 us -> 5.33 us
    all_gather x4 -> x0, waiting for transfers between devices: 74.3 us -> none  [the longest x1 43.5 us: local(): lax.all_gather(attended, 'mp', axis=1, tiled=True)]
    pallas_call x0 -> x1, Pallas kernels: none -> 46.3 us  [fused(): pl.pallas_call(functools.partial(fused_kernel, n), out_shape=jax.ShapeDty...]
    all_gather x3 -> x0, blocking collectives: 32 us -> none  [the longest x1 28 us: local(): lax.all_gather(mod_local, 'mp', axis=1, tiled=True)]
    dot_general x4 -> x0, matrix products: 8.38 us -> none  [the longest x1 3.95 us: local(): jnp.dot(modulated, qkv_full, preferred_element_type=jnp.float32)]
    unnamed x6 -> x8, local copies, waits for them, and re-layouts: 0.15 us -> 5.33 us
    reduce_sum x3 -> x0, other arithmetic: 3.94 us -> none  [the longest x1 1.96 us: layer_normed(): variance = jnp.mean(centred * centred, axis=-1, keepdims=True)]
    unnamed x4 -> x0, waiting for transfers between devices: 2.1 us -> none
  transfers between devices with their start and end apart: 4 -> 0, of which waited for: 4 -> 0; matrix products, arithmetic and copies ran while one was open for 8% -> 0% of each run, Pallas kernels for 0% -> 0%
where the time goes in v1:
time: 52.5 us; the launch traced here: 52.3 us
  Pallas kernels  46.3 us (88%)
  local copies, waits for them, and re-layouts  5.33 us (10%)
  between operations  0.67 us (1%)
    pallas_call x1, Pallas kernels, fused(): pl.pallas_call(functools.partial(fused_kernel, n), out_shape=jax.ShapeDty...  46.3 us
    unnamed x8, local copies, waits for them, and re-layouts  5.33 us

profile of v1, /device:TPU:0, one launch (start us, length us, event | category | flops | bytes accessed | tf_op | source)
XLA Modules:
  0.0 52.3 jit_solution(1338578414246718827)
XLA Ops:
  0.7 0.9 %copy.6.mod_ref = bf16[28,3,384]{2,1,0:T(4,128)(2,1)S(1)} copy(bf16[28,3,384]{2,0,1:T(8,128)(2,1)} %param.7) | data formatting | bytes 129024 | tf_op args[2]
  1.6 0.0 copy-start
  1.6 1.7 %copy-done = bf16[1536,768]{1,0:T(8,128)(2,1)S(1)} copy-done((bf16[1536,768]{1,0:T(8,128)(2,1)S(1)}, bf16[1536,768]{1,0:T(8,128)(2,1)}, u32[]{:S(2)}) %copy-start) | copy-done | bytes 2359320
  3.3 0.0 copy-start.1
  3.3 1.1 %copy-done.1 = bf16[1024,384]{1,0:T(8,128)(2,1)S(1)} copy-done((bf16[1024,384]{1,0:T(8,128)(2,1)S(1)}, bf16[1024,384]{1,0:T(8,128)(2,1)}, u32[]{:S(2)}) %copy-start.1) | copy-done | bytes 786456
  4.4 0.0 copy-start.2
  4.4 0.9 %copy-done.2 = bf16[256,384]{1,0:T(8,128)(2,1)S(1)} copy-done((bf16[256,384]{1,0:T(8,128)(2,1)S(1)}, bf16[256,384]{1,0:T(8,128)(2,1)}, u32[]{:S(2)}) %copy-start.2) | copy-done | bytes 196632
  5.3 46.3 %shard_map.55 = bf16[256,384]{1,0:T(8,128)(2,1)S(1)} custom-call(bf16[256,384]{1,0:T(8,128)(2,1)S(1)} %copy-done.2, s32[1]{0:T(128)S(6)} %copy.8.t_ref, bf16[28,3,384]{2,1,0:T(4,128)(2,1)S(1)} %copy.6.mod_ref, bf16[1536,768]{1,0:T(8,128)(2,1)S(1)} %copy-done, bf16[1024,384]{1,0:T(8,128)(2,1)S(1)} %copy-done.1), custom_call_target="tpu_custom_call" | custom-call | tf_op jit(solution)/shard_map/pallas_call | solution.py:423
  51.6 0.7 %copy.9 = bf16[256,384]{1,0:T(8,128)(2,1)} copy(bf16[256,384]{1,0:T(8,128)(2,1)S(1)} %shard_map.55) | data formatting | bytes 393216
Async XLA Ops:
  1.6 1.7 %copy-start = (bf16[1536,768]{1,0:T(8,128)(2,1)S(1)}, bf16[1536,768]{1,0:T(8,128)(2,1)}, u32[]{:S(2)}) copy-start(bf16[1536,768]{1,0:T(8,128)(2,1)} %wq_hbm.1) | copy-start | bytes 7077892
  3.3 1.1 %copy-start.1 = (bf16[1024,384]{1,0:T(8,128)(2,1)S(1)}, bf16[1024,384]{1,0:T(8,128)(2,1)}, u32[]{:S(2)}) copy-start(bf16[1024,384]{1,0:T(8,128)(2,1)} %wo_hbm.1) | copy-start | bytes 2359300
  4.4 0.9 %copy-start.2 = (bf16[256,384]{1,0:T(8,128)(2,1)S(1)}, bf16[256,384]{1,0:T(8,128)(2,1)}, u32[]{:S(2)}) copy-start(bf16[256,384]{1,0:T(8,128)(2,1)} %x_hbm.1) | copy-start | bytes 589828

commit v2 on v1

--- a/solution.py
+++ b/solution.py
@@ -95,11 +95,12 @@
     n,
     x_hbm,
     t_ref,
-    mod_ref,
+    mod_hbm,
     wq_hbm,
     wo_hbm,
     out_ref,
     xs,
+    table,
     small,
     wq,
     wo,
@@ -110,6 +111,7 @@
     att,
     mixed,
     own_sem,
+    table_sem,
     ssem,
     rsem,
     small_send,
@@ -135,6 +137,8 @@
 
     own_copy = pltpu.make_async_copy(x_hbm, xs.at[me], own_sem)
     own_copy.start()
+    table_copy = pltpu.make_async_copy(mod_hbm, table, table_sem)
+    table_copy.start()
 
     barrier = pltpu.get_barrier_semaphore()
     for step in range(1, n):
@@ -163,14 +167,21 @@
 
     own_copy.wait()
     mine = xs[me].astype(jnp.float32)
-    mod_f = mod_ref[t_ref[0]].astype(jnp.float32)
+    table_copy.wait()
+
+    def mod_row(j):
+        entries = table[j].astype(jnp.float32)
+        steps = lax.broadcasted_iota(jnp.int32, entries.shape, 0)
+        chosen = jnp.where(steps == t_ref[0], entries, 0.0)
+        return jnp.sum(chosen, axis=0, keepdims=True)
+
     mean_col = jnp.sum(mine, axis=1, keepdims=True) * (1.0 / feats)
     off = mine - mean_col
     m2_col = jnp.sum(off * off, axis=1, keepdims=True)
     mean_row = jnp.broadcast_to(mean_col, (rows, LANES)).T[0:1, :]
     m2_row = jnp.broadcast_to(m2_col, (rows, LANES)).T[0:1, :]
-    small[me, 0:1, :] = mod_f[0:1]
-    small[me, 1:2, :] = 1.0 + mod_f[1:2]
+    small[me, 0:1, :] = mod_row(0)
+    small[me, 1:2, :] = 1.0 + mod_row(1)
     small[me, 2:3, 0:rows] = mean_row
     small[me, 3:4, 0:rows] = m2_row
 
@@ -388,7 +399,7 @@
 
     sweep(1, use_mix)
 
-    gate = mod_ref[t_ref[0]].astype(jnp.float32)[2:3]
+    gate = mod_row(2)
     out_ref[...] = (xs[me].astype(jnp.float32) + gate * mixed[...]).astype(jnp.bfloat16)
 
     for step in range(1, n):
@@ -414,6 +425,7 @@
 
 
 def fused(n, latent, t_index, mod_table, w_qkv, w_out):
+    mod_table = jnp.transpose(mod_table, (1, 0, 2))
     rows, feats = latent.shape
     depth, cols = w_qkv.shape
     depth_o, cols_o = w_out.shape
@@ -424,15 +436,16 @@
         functools.partial(fused_kernel, n),
         out_shape=jax.ShapeDtypeStruct((rows, feats), bf),
         in_specs=[
-            pl.BlockSpec(memory_space=pl.ANY),
+            pl.BlockSpec(memory_space=pltpu.HBM),
             pl.BlockSpec(memory_space=pltpu.SMEM),
-            pl.BlockSpec(memory_space=pltpu.VMEM),
-            pl.BlockSpec(memory_space=pl.ANY),
-            pl.BlockSpec(memory_space=pl.ANY),
+            pl.BlockSpec(memory_space=pltpu.HBM),
+            pl.BlockSpec(memory_space=pltpu.HBM),
+            pl.BlockSpec(memory_space=pltpu.HBM),
         ],
         out_specs=pl.BlockSpec(memory_space=pltpu.VMEM),
         scratch_shapes=[
             pltpu.VMEM((n, rows, feats), bf),
+            pltpu.VMEM(mod_table.shape, bf),
             pltpu.VMEM((n, 8, feats), f32),
             pltpu.VMEM((n, 2 * depth // n, cols), bf),
             pltpu.VMEM((n, 2 * depth_o // n, cols_o), bf),
@@ -442,6 +455,7 @@
             pltpu.VMEM((heads, rows, 2 * HEAD_DIM), bf),
             pltpu.VMEM((n, rows, heads * HEAD_DIM), bf),
             pltpu.VMEM((rows, cols_o), f32),
+            dma,
             dma,
             dma((2, 3, n, 2)),
             dma((2, n, 2)),
@@ -455,7 +469,7 @@
             dma((heads,)),
         ],
         compiler_params=pltpu.CompilerParams(
-            collective_id=0, has_side_effects=True, vmem_limit_bytes=48 * 1024 * 1024
+            collective_id=0, has_side_effects=True, vmem_limit_bytes=60 * 1024 * 1024
         ),
     )(latent, t_index, mod_table, w_qkv, w_out)
 

time: 52.5 us -> 49.2 us (0.937)
  local copies, waits for them, and re-layouts: 5.33 us -> 1.62 us
    unnamed x8 -> x1, local copies, waits for them, and re-layouts: 5.33 us -> 1.62 us
where the time goes in v2:
time: 49.2 us; the launch traced here: 49 us
  Pallas kernels  46.7 us (95%)
  local copies, waits for them, and re-layouts  1.62 us (3%)
  between operations  0.66 us (1%)
    pallas_call x1, Pallas kernels, fused(): pl.pallas_call(functools.partial(fused_kernel, n), out_shape=jax.ShapeDty...  46.7 us
    unnamed x1, local copies, waits for them, and re-layouts  1.62 us

profile of v2, /device:TPU:0, one launch (start us, length us, event | category | flops | bytes accessed | tf_op | source)
XLA Modules:
  0.0 49.0 jit_solution(11334730071033520183)
XLA Ops:
  0.7 46.7 %shard_map.55 = bf16[256,384]{1,0:T(8,128)(2,1)} custom-call(bf16[256,384]{1,0:T(8,128)(2,1)} %x_hbm.1, s32[1]{0:T(128)S(6)} %copy.7.t_ref, bf16[3,28,384]{2,1,0:T(8,128)(2,1)} %bitcast.1, bf16[1536,768]{1,0:T(8,128)(2,1)} %wq_hbm.1, bf16[1024,384]{1,0:T(8,128)(2,1)} %wo_hbm.1), custom_call_target="tpu_custom_call" | custom-call | tf_op jit(solution)/shard_map/pallas_call | solution.py:435
  47.4 1.6 %copy.8 = bf16[256,384]{1,0:T(8,128)(2,1)} copy(bf16[256,384]{1,0:T(8,128)(2,1)} %shard_map.55) | data formatting | bytes 393216

commit v3 on v2

--- a/solution.py
+++ b/solution.py
@@ -275,6 +275,52 @@
     for i in range(per_sec):
         wo_remote(i).start()
 
+    def receive(phase, d):
+        where = []
+        for col in (True, False):
+            for sign in (1, -1):
+                sz = z + sign * (d if col else d - 1)
+                there = jnp.logical_and(sz >= 0, sz < deep)
+                if not col and sign < 0:
+                    there = jnp.logical_and(there, d > 1)
+                where.append((sz * WIDE + (x if col else 1 - x), there))
+        for h in range(2):
+            for src, there in where:
+
+                @pl.when(there)
+                def _():
+                    arrive(phase, src, h)
+
+    def consume(d, use):
+        def one(i, carry_in):
+            col = i < 2
+            sign = 1 - 2 * lax.rem(i, 2)
+            sz = z + sign * jnp.where(col, d, d - 1)
+            there = jnp.logical_and(sz >= 0, sz < deep)
+            there = jnp.logical_and(there, jnp.logical_or(i < 3, d > 1))
+            src = sz * WIDE + jnp.where(col, x, 1 - x)
+
+            @pl.when(there)
+            def _():
+                use(src)
+
+            return carry_in
+
+        lax.fori_loop(0, 4, one, 0)
+
+    def sweep(phase, use):
+        def early(d, carry):
+            receive(phase, d)
+            consume(d - 1, use)
+            return carry
+
+        lax.fori_loop(2, deep, early, 0)
+        consume(deep - 1, use)
+        receive(phase, deep)
+        consume(deep, use)
+
+    receive(0, 1)
+
     for step in range(1, n):
         p = lax.rem(me + step, n)
         pltpu.make_async_copy(small.at[p], small.at[p], small_recv.at[p]).wait()
@@ -309,41 +355,6 @@
 
     acc[...] = project(me)
 
-    def sweep(phase, use):
-        def body(d, carry):
-            where = []
-            for col in (True, False):
-                for sign in (1, -1):
-                    sz = z + sign * (d if col else d - 1)
-                    there = jnp.logical_and(sz >= 0, sz < deep)
-                    if not col and sign < 0:
-                        there = jnp.logical_and(there, d > 1)
-                    where.append((sz * WIDE + (x if col else 1 - x), there))
-            for h in range(2):
-                for src, there in where:
-
-                    @pl.when(there)
-                    def _():
-                        arrive(phase, src, h)
-
-            def one(i, carry_in):
-                col = i < 2
-                sign = 1 - 2 * lax.rem(i, 2)
-                sz = z + sign * jnp.where(col, d, d - 1)
-                there = jnp.logical_and(sz >= 0, sz < deep)
-                there = jnp.logical_and(there, jnp.logical_or(i < 3, d > 1))
-                src = sz * WIDE + jnp.where(col, x, 1 - x)
-
-                @pl.when(there)
-                def _():
-                    use(src)
-
-                return carry_in
-
-            return lax.fori_loop(0, 4, one, carry)
-
-        lax.fori_loop(1, deep + 1, body, 0)
-
     def use_projection(src):
         acc[...] += project(src)
 
@@ -392,6 +403,7 @@
         pltpu.make_async_copy(wo.at[src], wo.at[src], wo_sem.at[src]).wait()
         return jnp.dot(att[src], wo[src], preferred_element_type=jnp.float32)
 
+    receive(1, 1)
     mixed[...] = mix(me)
 
     def use_mix(src):

time: 49.2 us -> 49.1 us (level)
  no operation moved by 1% of the time
where the time goes in v3:
time: 49.1 us; the launch traced here: 49 us
  Pallas kernels  46.7 us (95%)
  local copies, waits for them, and re-layouts  1.62 us (3%)
  between operations  0.66 us (1%)
    pallas_call x1, Pallas kernels, fused(): pl.pallas_call(functools.partial(fused_kernel, n), out_shape=jax.ShapeDty...  46.7 us
    unnamed x1, local copies, waits for them, and re-layouts  1.62 us

profile of v3, /device:TPU:0, one launch (start us, length us, event | category | flops | bytes accessed | tf_op | source)
XLA Modules:
  0.0 49.0 jit_solution(8494241697153407800)
XLA Ops:
  0.7 46.7 %shard_map.55 = bf16[256,384]{1,0:T(8,128)(2,1)} custom-call(bf16[256,384]{1,0:T(8,128)(2,1)} %x_hbm.1, s32[1]{0:T(128)S(6)} %copy.7.t_ref, bf16[3,28,384]{2,1,0:T(8,128)(2,1)} %bitcast.1, bf16[1536,768]{1,0:T(8,128)(2,1)} %wq_hbm.1, bf16[1024,384]{1,0:T(8,128)(2,1)} %wo_hbm.1), custom_call_target="tpu_custom_call" | custom-call | tf_op jit(solution)/shard_map/pallas_call | solution.py:447
  47.4 1.6 %copy.8 = bf16[256,384]{1,0:T(8,128)(2,1)} copy(bf16[256,384]{1,0:T(8,128)(2,1)} %shard_map.55) | data formatting | bytes 393216

commit v4 on v3

--- a/solution.py
+++ b/solution.py
@@ -11,6 +11,7 @@
 HEAD_DIM = 128
 LANES = 128
 WIDE = 2
+CHUNKS = (2, 2)
 MESH = pl.DeviceIdType.MESH
 
 
@@ -129,7 +130,6 @@
     deep = n // WIDE
     z, x = me // WIDE, me % WIDE
     rows, feats = x_hbm.shape
-    half = rows // 2
     piece_q = wq.shape[1]
     per_sec = n // 2
     piece_o = wo.shape[1]
@@ -199,22 +199,20 @@
 
     def chunk(phase, src, h):
         if phase == 0:
-            return xs.at[src, pl.ds(h * half, half), :]
-        return att.at[src, :, pl.ds(h * HEAD_DIM, HEAD_DIM)]
-
-    def route(src, h):
+            part = rows // CHUNKS[0]
+            return xs.at[src, pl.ds(h * part, part), :]
+        split = CHUNKS[1] // heads
+        part = rows // split
+        return att.at[
+            src, pl.ds(h % split * part, part), pl.ds(h // split * HEAD_DIM, HEAD_DIM)
+        ]
+
+    def route(src):
         sz, sx = src // WIDE, src % WIDE
         same = sx == x
-        if h == 0:
-            first = jnp.bool_(False)
-        else:
-            first = jnp.logical_or(sz == 0, sz == deep - 1)
-        flow = jnp.logical_or(same, first)
-        up = jnp.logical_and(flow, jnp.logical_and(sz <= z, z + 1 < deep))
-        down = jnp.logical_and(flow, jnp.logical_and(sz >= z, z > 0))
-        across = jnp.logical_and(
-            same, jnp.logical_or(jnp.logical_not(first), sz == z)
-        )
+        up = jnp.logical_and(same, jnp.logical_and(sz <= z, z + 1 < deep))
+        down = jnp.logical_and(same, jnp.logical_and(sz >= z, z > 0))
+        across = same
         return (
             (0, up, me + WIDE),
             (1, down, me - WIDE),
@@ -232,7 +230,7 @@
         )
 
     def relay(phase, src, h):
-        for direction, wanted, target in route(src, h):
+        for direction, wanted, target in route(src):
 
             @pl.when(wanted)
             def _():
@@ -242,11 +240,10 @@
         hop(phase, src, h, 0, me).wait_recv()
         relay(phase, src, h)
 
-    for h in range(2):
+    for step in range(1, n):
+        small_copy(step).start()
+    for h in range(CHUNKS[0]):
         relay(0, me, h)
-        if h == 0:
-            for step in range(1, n):
-                small_copy(step).start()
 
     def wq_remote(i):
         p = sec * per_sec + i
@@ -277,21 +274,17 @@
 
     def receive(phase, d):
         where = []
-        for col in (True, False):
-            for sign in (1, -1):
-                sz = z + sign * (d if col else d - 1)
-                there = jnp.logical_and(sz >= 0, sz < deep)
-                if not col and sign < 0:
-                    there = jnp.logical_and(there, d > 1)
-                where.append((sz * WIDE + (x if col else 1 - x), there))
-        for h in range(2):
+        for sign in (1, -1):
+            sz = z + sign * d
+            where.append((sz * WIDE + x, jnp.logical_and(sz >= 0, sz < deep)))
+        for h in range(CHUNKS[phase]):
             for src, there in where:
 
                 @pl.when(there)
                 def _():
                     arrive(phase, src, h)
 
-    def consume(d, use):
+    def consume(phase, d, use):
         def one(i, carry_in):
             col = i < 2
             sign = 1 - 2 * lax.rem(i, 2)
@@ -300,6 +293,11 @@
             there = jnp.logical_and(there, jnp.logical_or(i < 3, d > 1))
             src = sz * WIDE + jnp.where(col, x, 1 - x)
 
+            @pl.when(jnp.logical_and(there, i >= 2))
+            def _():
+                for h in range(CHUNKS[phase]):
+                    hop(phase, src, h, 0, me).wait_recv()
+
             @pl.when(there)
             def _():
                 use(src)
@@ -311,13 +309,12 @@
     def sweep(phase, use):
         def early(d, carry):
             receive(phase, d)
-            consume(d - 1, use)
+            consume(phase, d - 1, use)
             return carry
 
         lax.fori_loop(2, deep, early, 0)
-        consume(deep - 1, use)
-        receive(phase, deep)
-        consume(deep, use)
+        consume(phase, deep - 1, use)
+        consume(phase, deep, use)
 
     receive(0, 1)
 
@@ -397,7 +394,8 @@
             e_own.astype(jnp.bfloat16), own_v, preferred_element_type=jnp.float32
         ) + jnp.dot(e_far.astype(jnp.bfloat16), far_v, preferred_element_type=jnp.float32)
         att[me, :, h * HEAD_DIM : (h + 1) * HEAD_DIM] = (weighted / norm).astype(jnp.bfloat16)
-        relay(1, me, h)
+        for c in range(CHUNKS[1] // heads):
+            relay(1, me, h * (CHUNKS[1] // heads) + c)
 
     def mix(src):
         pltpu.make_async_copy(wo.at[src], wo.at[src], wo_sem.at[src]).wait()
@@ -424,8 +422,8 @@
 
     def drain(src, carry):
         for phase in range(2):
-            for h in range(2):
-                for direction, wanted, target in route(src, h):
+            for h in range(CHUNKS[phase]):
+                for direction, wanted, target in route(src):
 
                     @pl.when(wanted)
                     def _():
@@ -469,8 +467,8 @@
             pltpu.VMEM((rows, cols_o), f32),
             dma,
             dma,
-            dma((2, 3, n, 2)),
-            dma((2, n, 2)),
+            dma((2, 3, n, max(CHUNKS))),
+            dma((2, n, max(CHUNKS))),
             dma((n,)),
             dma((n,)),
             dma((n,)),

time: 49.1 us -> 47.3 us (0.963)
  Pallas kernels: 46.7 us -> 44.9 us
    pallas_call x1, Pallas kernels: 46.7 us -> 44.9 us  [fused(): pl.pallas_call(functools.partial(fused_kernel, n), out_shape=jax.ShapeDty...]
where the time goes in v4:
time: 47.3 us; the launch traced here: 47.2 us
  Pallas kernels  44.9 us (95%)
  local copies, waits for them, and re-layouts  1.62 us (3%)
  between operations  0.66 us (1%)
    pallas_call x1, Pallas kernels, fused(): pl.pallas_call(functools.partial(fused_kernel, n), out_shape=jax.ShapeDty...  44.9 us
    unnamed x1, local copies, waits for them, and re-layouts  1.62 us

profile of v4, /device:TPU:0, one launch (start us, length us, event | category | flops | bytes accessed | tf_op | source)
XLA Modules:
  0.0 47.2 jit_solution(3419635709106671441)
XLA Ops:
  0.7 44.9 %shard_map.55 = bf16[256,384]{1,0:T(8,128)(2,1)} custom-call(bf16[256,384]{1,0:T(8,128)(2,1)} %x_hbm.1, s32[1]{0:T(128)S(6)} %copy.7.t_ref, bf16[3,28,384]{2,1,0:T(8,128)(2,1)} %bitcast.1, bf16[1536,768]{1,0:T(8,128)(2,1)} %wq_hbm.1, bf16[1024,384]{1,0:T(8,128)(2,1)} %wo_hbm.1), custom_call_target="tpu_custom_call" | custom-call | tf_op jit(solution)/shard_map/pallas_call | solution.py:445
  45.5 1.6 %copy.8 = bf16[256,384]{1,0:T(8,128)(2,1)} copy(bf16[256,384]{1,0:T(8,128)(2,1)} %shard_map.55) | data formatting | bytes 393216

commit v5 on v4

--- a/solution.py
+++ b/solution.py
@@ -214,9 +214,9 @@
         down = jnp.logical_and(same, jnp.logical_and(sz >= z, z > 0))
         across = same
         return (
+            (2, across, z * WIDE + (1 - x)),
             (0, up, me + WIDE),
             (1, down, me - WIDE),
-            (2, across, z * WIDE + (1 - x)),
         )
 
     def hop(phase, src, h, direction, target):
@@ -240,9 +240,10 @@
         hop(phase, src, h, 0, me).wait_recv()
         relay(phase, src, h)
 
+    relay(0, me, 0)
     for step in range(1, n):
         small_copy(step).start()
-    for h in range(CHUNKS[0]):
+    for h in range(1, CHUNKS[0]):
         relay(0, me, h)
 
     def wq_remote(i):

time: 47.3 us -> 47.1 us (level)
  no operation moved by 1% of the time
where the time goes in v5:
time: 47.1 us; the launch traced here: 46.9 us
  Pallas kernels  44.7 us (95%)
  local copies, waits for them, and re-layouts  1.62 us (3%)
  between operations  0.66 us (1%)
    pallas_call x1, Pallas kernels, fused(): pl.pallas_call(functools.partial(fused_kernel, n), out_shape=jax.ShapeDty...  44.7 us
    unnamed x1, local copies, waits for them, and re-layouts  1.62 us

profile of v5, /device:TPU:0, one launch (start us, length us, event | category | flops | bytes accessed | tf_op | source)
XLA Modules:
  0.0 46.9 jit_solution(955550869468892710)
XLA Ops:
  0.7 44.7 %shard_map.55 = bf16[256,384]{1,0:T(8,128)(2,1)} custom-call(bf16[256,384]{1,0:T(8,128)(2,1)} %x_hbm.1, s32[1]{0:T(128)S(6)} %copy.7.t_ref, bf16[3,28,384]{2,1,0:T(8,128)(2,1)} %bitcast.1, bf16[1536,768]{1,0:T(8,128)(2,1)} %wq_hbm.1, bf16[1024,384]{1,0:T(8,128)(2,1)} %wo_hbm.1), custom_call_target="tpu_custom_call" | custom-call | tf_op jit(solution)/shard_map/pallas_call | solution.py:446
  45.3 1.6 %copy.8 = bf16[256,384]{1,0:T(8,128)(2,1)} copy(bf16[256,384]{1,0:T(8,128)(2,1)} %shard_map.55) | data formatting | bytes 393216

commit v6 on v5

--- a/solution.py
+++ b/solution.py
@@ -375,12 +375,17 @@
 
     factor = 1.0 / math.sqrt(HEAD_DIM)
     contract = (((1,), (1,)), ((), ()))
+    near = []
     for h in range(heads):
         base = 3 * h * HEAD_DIM
         queries = acc[:, base : base + HEAD_DIM].astype(jnp.bfloat16)
         own_k = proj[:, base + HEAD_DIM : base + 2 * HEAD_DIM]
+        s_own = lax.dot_general(queries, own_k, contract, preferred_element_type=jnp.float32) * factor
+        near.append((queries, s_own))
+    for h in range(heads):
+        base = 3 * h * HEAD_DIM
+        queries, s_own = near[h]
         own_v = proj[:, base + 2 * HEAD_DIM : base + 3 * HEAD_DIM]
-        s_own = lax.dot_general(queries, own_k, contract, preferred_element_type=jnp.float32) * factor
         kv_copy(h).wait_recv()
         far_k = pkv[h, :, 0:HEAD_DIM]
         far_v = pkv[h, :, HEAD_DIM : 2 * HEAD_DIM]

time: 47.1 us -> 47.1 us (level)
  no operation moved by 1% of the time
where the time goes in v6:
time: 47.1 us; the launch traced here: 46.9 us
  Pallas kernels  44.7 us (95%)
  local copies, waits for them, and re-layouts  1.62 us (3%)
  between operations  0.66 us (1%)
    pallas_call x1, Pallas kernels, fused(): pl.pallas_call(functools.partial(fused_kernel, n), out_shape=jax.ShapeDty...  44.7 us
    unnamed x1, local copies, waits for them, and re-layouts  1.62 us

profile of v6, /device:TPU:0, one launch (start us, length us, event | category | flops | bytes accessed | tf_op | source)
XLA Modules:
  0.0 46.9 jit_solution(13347456415041016592)
XLA Ops:
  0.7 44.7 %shard_map.55 = bf16[256,384]{1,0:T(8,128)(2,1)} custom-call(bf16[256,384]{1,0:T(8,128)(2,1)} %x_hbm.1, s32[1]{0:T(128)S(6)} %copy.7.t_ref, bf16[3,28,384]{2,1,0:T(8,128)(2,1)} %bitcast.1, bf16[1536,768]{1,0:T(8,128)(2,1)} %wq_hbm.1, bf16[1024,384]{1,0:T(8,128)(2,1)} %wo_hbm.1), custom_call_target="tpu_custom_call" | custom-call | tf_op jit(solution)/shard_map/pallas_call | solution.py:451
  45.3 1.6 %copy.8 = bf16[256,384]{1,0:T(8,128)(2,1)} copy(bf16[256,384]{1,0:T(8,128)(2,1)} %shard_map.55) | data formatting | bytes 393216
